TPU v7x, 32 devices: a whole 2x2x4 slice. The times are simulated.
32 devices in a mesh: mode: 8 (over z, y), tm: 4 (over x, core).
Axes of the slice: x: 2, y: 2, z: 4, core: 2. Of those that a mesh axis runs over, the one named last changes fastest.
Arguments:
- support_accel: bfloat16 [512, 2048], P(None, 'tm'), may hold values from -6 to 6
- participation: bfloat16 [2048, 512], P('mode'), may hold values from -0.25 to 0.25
- kernels: float32 [2048, 2048], P('mode'), may hold values from -0.25 to 0.25
- lengths: int32 [2048], P('mode'), may hold values from 1 to 2048, as said below
- mode_shapes: bfloat16 [16384, 2048], P('mode'), may hold values from -0.125 to 0.125
- groups: int32 [16384], P('mode'), may hold values from 0 to 511
Outputs:
- response: bfloat16 [16384, 2048], P('mode', 'tm')
Inputs may be any that keep to these rules, and one draw needn't show every extreme that they name: `lengths`: some mode has exactly 2048 taps in every draw.
All inputs are finite; a program needn't handle non-finite values.
Results may differ from a plain program's by a relative error of at most 0.0033.
Values may be sent and summed in bfloat16 or wider, within the bound.
A program may use at most 64 MiB of HBM per device.

v0:
```python
import jax
import jax.numpy as jnp
from jax import lax
from jax.sharding import PartitionSpec as P


def passed_along(block, axis, distance):
    devices = range(lax.axis_size(axis))
    route = [(i - distance, i) for i in devices if i - distance in devices]
    return lax.ppermute(block, axis, route)


def depthwise(signal, weights):
    flipped = jnp.flip(weights, 1)[:, None, :]
    result = lax.conv_general_dilated(
        signal[None],
        flipped,
        (1,),
        "VALID",
        dimension_numbers=("NCH", "OIH", "NCH"),
        feature_group_count=signal.shape[0],
        precision=lax.Precision.HIGHEST,
    )
    return result[0]


def apply_filter(signal, kernel):
    return depthwise(signal, kernel)


def per_device(support_accel, participation, kernels, lengths, mode_shapes, groups):
    slab_len = support_accel.shape[1]
    tap_count = kernels.shape[1]
    depth_slabs = tap_count // slab_len
    forces = jnp.dot(participation, support_accel, preferred_element_type=jnp.float32)
    alive = jnp.arange(tap_count, dtype=jnp.int32)[None, :] < lengths[:, None]
    masked = jnp.where(alive, kernels, jnp.zeros_like(kernels))
    pieces = [forces]
    for distance in range(1, depth_slabs + 1):
        pieces.insert(0, passed_along(forces, "tm", distance))
    window = jnp.concatenate(pieces, axis=1)
    modal = apply_filter(window[:, 1:], masked).astype(jnp.bfloat16)
    initial = jnp.zeros((mode_shapes.shape[0], slab_len), jnp.float32)
    piece = jax.tree.map(lambda part: lax.all_gather(part, "mode", axis=0, tiled=True), modal)
    columns = lax.slice_in_dim(mode_shapes, 0, piece.shape[0], axis=1)
    summed = initial + jnp.dot(columns, piece, preferred_element_type=jnp.float32)
    ground = jnp.take(support_accel, groups, axis=0).astype(jnp.float32)
    return (summed + ground).astype(jnp.bfloat16)


def solution(mesh):
    placed = (
        P(None, "tm"),
        P("mode", None),
        P("mode", None),
        P("mode"),
        P("mode", None),
        P("mode"),
    )
    return jax.shard_map(
        per_device, mesh=mesh, in_specs=placed, out_specs=P("mode", "tm"), check_vma=False
    )
```

profile of v0, /device:TPU:0, one launch (start us, length us, event | category | flops | bytes accessed | tf_op | source)
XLA Modules:
  0.0 271.4 jit_solution(18268262673586640301)
XLA Ops:
  6.5 0.0 copy-start
  6.5 0.0 all-gather.3.cloned.1.call-start
  6.5 1.0 copy-done
  7.6 1.2 fusion.4
  8.8 1.5 collective-permute-start
  10.3 5.1 %collective-permute-start.1 = (f32[256,512]{1,0:T(8,128)S(1)}, f32[256,512]{1,0:T(8,128)}, u32[]{:S(2)}, u32[]{:S(2)}) collective-permute-start(f32[256,512]{1,0:T(8,128)S(1)} %fusion.4), channel_id=1, source_target_pairs={{0,3},{4,7},{8,11},{12,15},{16,19},{20,23},{24,27},{28,31}} | collective-permute-start | bytes 1572872 | tf_op jit(solution)/shard_map/ppermute | solution.py:10
  15.4 2.1 collective-permute-start.2
  17.5 2.1 collective-permute-start.3
  19.6 1.8 fusion.2
  21.4 11.6 %rev.4 = f32[256,2048]{1,0:T(8,128)} reverse(f32[256,2048]{1,0:T(8,128)S(1)} %fusion.2), dimensions={1} | reverse | bytes 4194304 | tf_op jit(solution)/shard_map/jit(_flip)/rev | solution.py:14
  33.0 6.1 %copy.12 = f32[256,1,2048]{0,1,2:T(1,128)} copy(f32[256,1,2048]{2,0,1:T(8,128)} %bitcast.15) | data formatting | bytes 4194304 | tf_op jit(solution)/shard_map/broadcast_in_dim | solution.py:14
  39.1 0.0 collective-permute-done
  39.1 1.1 constant_dynamic-update-slice_fusion.4
  40.2 0.0 collective-permute-done.1
  40.2 1.1 constant_dynamic-update-slice_fusion.3
  41.3 0.0 collective-permute-done.2
  41.3 1.1 constant_dynamic-update-slice_fusion.2
  42.3 0.0 collective-permute-done.3
  42.4 1.1 constant_dynamic-update-slice_fusion.1
  43.5 0.8 slice_bitcast_fusion
  44.2 4.0 %copy.11 = f32[1,256,2559]{1,0,2:T(1,128)} copy(f32[1,256,2559]{2,1,0:T(8,128)S(1)} %slice_bitcast_fusion) | data formatting | bytes 5240832 | tf_op jit(solution)/shard_map/broadcast_in_dim | solution.py:16
  48.3 0.0 copy-start.1
  48.3 90.9 %convolution_convert_fusion = bf16[1,256,512]{1,0,2:T(2,128)(2,1)} fusion(f32[1,256,2559]{1,0,2:T(1,128)} %copy.11, f32[256,1,2048]{0,1,2:T(1,128)} %copy.12), kind=kOutput, calls=%fused_computation.7 | convolution fusion | flops 3221356544 | bytes 4979712 | tf_op jit(solution)/shard_map/conv_general_dilated | solution.py:15
  139.1 0.0 all-gather.3.cloned.1.call-update
  139.2 0.0 copy-done.1
  139.2 7.5 %gather_fusion = bf16[2048,512]{1,0:T(8,128)(2,1)S(1)} fusion(bf16[512,512]{1,0:T(8,128)(2,1)S(1)} %copy-done, s32[2048]{0:T(1024)S(1)} %fusion.3), kind=kCustom, calls=%fused_computation | custom fusion | bytes 4202496 | tf_op jit(solution)/shard_map/jit(_take)/gather | solution.py:47
  146.7 2.4 copy.14
  149.1 92.8 %all-gather.3.cloned.1.call-done = bf16[1,2048,512]{1,0,2:T(2,128)(2,1)} async-done(((bf16[1,256,512]{1,0,2:T(2,128)(2,1)}), bf16[1,2048,512]{1,0,2:T(2,128)(2,1)}) %all-gather.3.cloned.1.call-update) | async-done | bytes 2097168 | tf_op jit(solution)/shard_map/all_gather | solution.py:44
  241.9 9.0 %copy.13 = bf16[1,2048,512]{2,1,0:T(8,128)(2,1)S(1)} copy(bf16[1,2048,512]{1,0,2:T(2,128)(2,1)} %all-gather.3.cloned.1.call-done) | data formatting | bytes 4194304 | tf_op jit(solution)/shard_map/all_gather | solution.py:44
  250.9 9.7 %fusion = bf16[2048,512]{0,1:T(8,128)(2,1)} fusion(bf16[2048,2048]{1,0:T(8,128)(2,1)} %param.10, bf16[1,2048,512]{2,1,0:T(8,128)(2,1)S(1)} %copy.13, bf16[2048,512]{0,1:T(8,128)(2,1)} %copy.14, pred[2048]{0:T(1024)(128)(4,1)S(1)} %compare_and_fusion), kind=kOutput, calls=%fused_computation.2 | convolution fusion | flops 4299161600 | bytes 14682112 | tf_op jit(solution)/shard_map/dot_general | solution.py:46
  260.6 3.9 %copy.15 = bf16[2048,512]{1,0:T(8,128)(2,1)} copy(bf16[2048,512]{0,1:T(8,128)(2,1)} %fusion) | data formatting | bytes 4194304 | tf_op jit(solution)/shard_map/convert_element_type | solution.py:48
  (3 shorter events, 0.1 us)
Async XLA Ops:
  6.5 1.0 copy-start
  6.5 235.4 %all-gather.3.cloned.1.call-start = ((), (), s32[]{:S(2)}) async-start(), calls=%async_computation | async-start | bytes 4718592 | tf_op jit(solution)/shard_map/all_gather | solution.py:44
  8.8 30.3 %collective-permute-start = (f32[256,512]{1,0:T(8,128)S(1)}, f32[256,512]{1,0:T(8,128)}, u32[]{:S(2)}, u32[]{:S(2)}) collective-permute-start(f32[256,512]{1,0:T(8,128)S(1)} %fusion.4), channel_id=1, source_target_pairs={} | collective-permute-start | bytes 1572872 | tf_op jit(solution)/shard_map/ppermute | solution.py:10
  10.3 29.9 %collective-permute-start.1 = (f32[256,512]{1,0:T(8,128)S(1)}, f32[256,512]{1,0:T(8,128)}, u32[]{:S(2)}, u32[]{:S(2)}) collective-permute-start(f32[256,512]{1,0:T(8,128)S(1)} %fusion.4), channel_id=1, source_target_pairs={{0,3},{4,7},{8,11},{12,15},{16,19},{20,23},{24,27},{28,31}} | collective-permute-start | bytes 1572872 | tf_op jit(solution)/shard_map/ppermute | solution.py:10
  15.4 25.9 %collective-permute-start.2 = (f32[256,512]{1,0:T(8,128)S(1)}, f32[256,512]{1,0:T(8,128)}, u32[]{:S(2)}, u32[]{:S(2)}) collective-permute-start(f32[256,512]{1,0:T(8,128)S(1)} %fusion.4), channel_id=1, source_target_pairs={{0,2},{1,3},{4,6},{5,7},{8,10},{9,11},{12,14},{13,15},{16,18},{17,... | collective-permute-start | bytes 1572872 | tf_op jit(solution)/shard_map/ppermute | solution.py:10
  17.5 24.9 %collective-permute-start.3 = (f32[256,512]{1,0:T(8,128)S(1)}, f32[256,512]{1,0:T(8,128)}, u32[]{:S(2)}, u32[]{:S(2)}) collective-permute-start(f32[256,512]{1,0:T(8,128)S(1)} %fusion.4), channel_id=1, source_target_pairs={{0,1},{1,2},{2,3},{4,5},{5,6},{6,7},{8,9},{9,10},{10,11},{12,13},{... | collective-permute-start | bytes 1572872 | tf_op jit(solution)/shard_map/ppermute | solution.py:10
  48.3 90.9 %copy-start.1 = (s32[2048]{0:T(1024)S(1)}, s32[2048]{0:T(1024)}, u32[]{:S(2)}) copy-start(s32[2048]{0:T(1024)} %param.11) | copy-start | bytes 24580
Sparse Core Ops, SparseCore 0:
  139.3 102.5 all-gather.2
where the time goes:
time: 272 us; the launch traced here: 271 us
  matrix products  102 us (38%)
  waiting for transfers between devices  92.8 us (34%)
  local copies, waits for them, and re-layouts  50.7 us (19%)
  between operations  13.5 us (5%)
  starting transfers between devices  10.8 us (4%)
    all_gather x1, waiting for transfers between devices, per_device(): lax.all_gather(part, 'mode', axis=0, tiled=True)  92.8 us
    conv_general_dilated x1, matrix products, depthwise(): lax.conv_general_dilated(signal[None], flipped, (1,), 'VALID', dimension_...  90.9 us
    rev x1, local copies, waits for them, and re-layouts, depthwise(): flipped = jnp.flip(weights, 1)[:, None, :]  11.6 us
    ppermute x4, starting transfers between devices, passed_along(): return lax.ppermute(block, axis, route)  10.7 us
    gather x2, local copies, waits for them, and re-layouts, per_device(): ground = jnp.take(support_accel, groups, axis=0).astype(jnp.float32)  9.92 us
    dot_general x1, matrix products, per_device(): jnp.dot(columns, piece, preferred_element_type=jnp.float32)  9.71 us
    all_gather x1, local copies, waits for them, and re-layouts, per_device(): lax.all_gather(part, 'mode', axis=0, tiled=True)  8.97 us
    broadcast_in_dim x1, local copies, waits for them, and re-layouts, depthwise(): flipped = jnp.flip(weights, 1)[:, None, :]  6.06 us
  transfers between devices with their start and end apart: 5, of which 1 were waited for; matrix products, arithmetic and copies ran while one was open for 12% of the time, Pallas kernels for 0%

commit v1 on v0

--- a/solution.py
+++ b/solution.py
@@ -2,6 +2,27 @@
 import jax.numpy as jnp
 from jax import lax
 from jax.sharding import PartitionSpec as P
+
+
+def gather_around(x, axis, dim):
+    size, index, rows = (lax.axis_size(axis), lax.axis_index(axis), x.shape[dim])
+    upward = [(i, (i + 1) % size) for i in range(size)]
+    behind = [(i, (i - 1) % size) for i in range(size)]
+    whole = jnp.zeros((*x.shape[:dim], size * rows, *x.shape[dim + 1 :]), x.dtype)
+    whole = lax.dynamic_update_slice_in_dim(whole, x, index * rows, axis=dim)
+    from_left = from_right = x
+    middle = size // 2
+    for step in range(1, middle + 1):
+        from_left = lax.ppermute(from_left, axis, upward)
+        whole = lax.dynamic_update_slice_in_dim(
+            whole, from_left, (index - step) % size * rows, axis=dim
+        )
+        if step < size - middle:
+            from_right = lax.ppermute(from_right, axis, behind)
+            whole = lax.dynamic_update_slice_in_dim(
+                whole, from_right, (index + step) % size * rows, axis=dim
+            )
+    return whole
 
 
 def passed_along(block, axis, distance):
@@ -41,7 +62,7 @@
     window = jnp.concatenate(pieces, axis=1)
     modal = apply_filter(window[:, 1:], masked).astype(jnp.bfloat16)
     initial = jnp.zeros((mode_shapes.shape[0], slab_len), jnp.float32)
-    piece = jax.tree.map(lambda part: lax.all_gather(part, "mode", axis=0, tiled=True), modal)
+    piece = jax.tree.map(lambda part: gather_around(part, "mode", 0), modal)
     columns = lax.slice_in_dim(mode_shapes, 0, piece.shape[0], axis=1)
     summed = initial + jnp.dot(columns, piece, preferred_element_type=jnp.float32)
     ground = jnp.take(support_accel, groups, axis=0).astype(jnp.float32)

time: 272 us -> 191 us (0.70)
  waiting for transfers between devices: 92.8 us -> 19.3 us
  starting transfers between devices: 10.8 us -> 28.6 us
  between operations: 13.5 us -> 0.21 us
  local copies, waits for them, and re-layouts: 50.7 us -> 42.4 us
  matrix products: 102 us -> 98.4 us
    all_gather x1 -> x0, waiting for transfers between devices: 92.8 us -> none  [per_device(): lax.all_gather(part, 'mode', axis=0, tiled=True)]
    ppermute x0 -> x7, waiting for transfers between devices: none -> 19.3 us  [the longest x4 12.3 us: gather_around(): from_left = lax.ppermute(from_left, axis, upward)]
    ppermute x0 -> x7, starting transfers between devices: none -> 17.9 us  [the longest x3 13.6 us: gather_around(): from_right = lax.ppermute(from_right, axis, behind)]
    all_gather x1 -> x0, local copies, waits for them, and re-layouts: 8.97 us -> none  [per_device(): lax.all_gather(part, 'mode', axis=0, tiled=True)]
  transfers between devices with their start and end apart: 5 -> 11, of which waited for: 1 -> 4; matrix products, arithmetic and copies ran while one was open for 12% -> 18% of each run, Pallas kernels for 0% -> 0%
where the time goes in v1:
time: 191 us
  matrix products  98.4 us (52%)
  local copies, waits for them, and re-layouts  42.4 us (22%)
  starting transfers between devices  28.6 us (15%)
  waiting for transfers between devices  19.3 us (10%)
    conv_general_dilated x1, matrix products, depthwise(): lax.conv_general_dilated(signal[None], flipped, (1,), 'VALID', dimension_...  88.7 us
    ppermute x3, starting transfers between devices, gather_around(): from_right = lax.ppermute(from_right, axis, behind)  13.6 us
    ppermute x4, waiting for transfers between devices, gather_around(): from_left = lax.ppermute(from_left, axis, upward)  12.3 us
    rev x1, local copies, waits for them, and re-layouts, depthwise(): flipped = jnp.flip(weights, 1)[:, None, :]  11.6 us
    ppermute x4, starting transfers between devices, passed_along(): return lax.ppermute(block, axis, route)  10.8 us
    gather x2, local copies, waits for them, and re-layouts, per_device(): ground = jnp.take(support_accel, groups, axis=0).astype(jnp.float32)  9.91 us
    dot_general x1, matrix products, per_device(): jnp.dot(columns, piece, preferred_element_type=jnp.float32)  8.39 us
    ppermute x3, waiting for transfers between devices, gather_around(): from_right = lax.ppermute(from_right, axis, behind)  7.01 us
  transfers between devices with their start and end apart: 11, of which 4 were waited for; matrix products, arithmetic and copies ran while one was open for 18% of the time, Pallas kernels for 0%

profile of v1, /device:TPU:0, one launch (start us, length us, event | category | flops | bytes accessed | tf_op | source)
XLA Modules:
  0.0 190.7 jit_solution(9105364130895350080)
XLA Ops:
  0.0 0.0 copy-start
  0.0 1.0 copy-done
  1.0 1.2 fusion.3
  2.3 1.5 collective-permute-start
  3.8 5.1 %collective-permute-start.1 = (f32[256,512]{1,0:T(8,128)S(1)}, f32[256,512]{1,0:T(8,128)}, u32[]{:S(2)}, u32[]{:S(2)}) collective-permute-start(f32[256,512]{1,0:T(8,128)S(1)} %fusion.3), channel_id=1, source_target_pairs={{0,3},{4,7},{8,11},{12,15},{16,19},{20,23},{24,27},{28,31}} | collective-permute-start | bytes 1572872 | tf_op jit(solution)/shard_map/ppermute | solution.py:31
  8.9 2.1 %collective-permute-start.2 = (f32[256,512]{1,0:T(8,128)S(1)}, f32[256,512]{1,0:T(8,128)}, u32[]{:S(2)}, u32[]{:S(2)}) collective-permute-start(f32[256,512]{1,0:T(8,128)S(1)} %fusion.3), channel_id=1, source_target_pairs={{0,2},{1,3},{4,6},{5,7},{8,10},{9,11},{12,14},{13,15},{16,18},{17,... | collective-permute-start | bytes 1572872 | tf_op jit(solution)/shard_map/ppermute | solution.py:31
  11.0 2.1 %collective-permute-start.3 = (f32[256,512]{1,0:T(8,128)S(1)}, f32[256,512]{1,0:T(8,128)}, u32[]{:S(2)}, u32[]{:S(2)}) collective-permute-start(f32[256,512]{1,0:T(8,128)S(1)} %fusion.3), channel_id=1, source_target_pairs={{0,1},{1,2},{2,3},{4,5},{5,6},{6,7},{8,9},{9,10},{10,11},{12,13},{... | collective-permute-start | bytes 1572872 | tf_op jit(solution)/shard_map/ppermute | solution.py:31
  13.0 1.8 fusion.1
  14.8 11.6 %rev.4 = f32[256,2048]{1,0:T(8,128)} reverse(f32[256,2048]{1,0:T(8,128)S(1)} %fusion.1), dimensions={1} | reverse | bytes 4194304 | tf_op jit(solution)/shard_map/jit(_flip)/rev | solution.py:35
  26.5 6.1 %copy.12 = f32[256,1,2048]{0,1,2:T(1,128)} copy(f32[256,1,2048]{2,0,1:T(8,128)} %bitcast.15) | data formatting | bytes 4194304 | tf_op jit(solution)/shard_map/broadcast_in_dim | solution.py:35
  32.5 0.0 collective-permute-done
  32.6 1.1 constant_dynamic-update-slice_fusion.4
  33.6 0.0 collective-permute-done.1
  33.6 1.1 constant_dynamic-update-slice_fusion.3
  34.7 0.0 collective-permute-done.2
  34.7 1.1 constant_dynamic-update-slice_fusion.2
  35.8 0.0 collective-permute-done.3
  35.8 1.1 constant_dynamic-update-slice_fusion.1
  37.0 0.8 slice_bitcast_fusion
  37.7 4.0 %copy.11 = f32[1,256,2559]{1,0,2:T(1,128)} copy(f32[1,256,2559]{2,1,0:T(8,128)S(1)} %slice_bitcast_fusion) | data formatting | bytes 5240832 | tf_op jit(solution)/shard_map/broadcast_in_dim | solution.py:37
  41.7 0.0 copy-start.2
  41.7 88.7 %convolution_convert_fusion = bf16[1,256,512]{1,0,2:T(2,128)(2,1)S(1)} fusion(f32[1,256,2559]{1,0,2:T(1,128)} %copy.11, f32[256,1,2048]{0,1,2:T(1,128)} %copy.12), kind=kOutput, calls=%fused_computation.6 | convolution fusion | flops 3221356544 | bytes 4979712 | tf_op jit(solution)/shard_map/conv_general_dilated | solution.py:36
  130.5 0.7 copy.13
  131.2 1.6 collective-permute-start.4
  132.7 3.2 %collective-permute-start.5 = (bf16[256,512]{1,0:T(8,128)(2,1)S(1)}, bf16[256,512]{1,0:T(8,128)(2,1)S(1)}, u32[]{:S(2)}, u32[]{:S(2)}) collective-permute-start(bf16[256,512]{1,0:T(8,128)(2,1)S(1)} %bitcast.17), channel_id=1, source_target_pairs={{0,28},{4,0},{8,4},{12,8},{16,12},{20,16},{24,20},{28,24},{1,29},{... | collective-permute-start | bytes 786440 | tf_op jit(solution)/shard_map/ppermute | solution.py:21
  135.9 0.0 copy-done.2
  135.9 7.3 %collective-permute-done.4 = bf16[256,512]{1,0:T(8,128)(2,1)} collective-permute-done((bf16[256,512]{1,0:T(8,128)(2,1)S(1)}, bf16[256,512]{1,0:T(8,128)(2,1)}, u32[]{:S(2)}, u32[]{:S(2)}) %collective-permute-start.4) | collective-permute-done | bytes 262176 | tf_op jit(solution)/shard_map/ppermute | solution.py:16
  143.2 2.6 %collective-permute-start.6 = (bf16[256,512]{1,0:T(8,128)(2,1)}, bf16[256,512]{1,0:T(8,128)(2,1)S(1)}, u32[]{:S(2)}, u32[]{:S(2)}) collective-permute-start(bf16[256,512]{1,0:T(8,128)(2,1)} %collective-permute-done.4), channel_id=1, source_target_pairs={{0,4},{4,8},{8,12},{12,16},{16,20},{20,24},{24,28},{28,0},{1,5},{5... | collective-permute-start | bytes 786440 | tf_op jit(solution)/shard_map/ppermute | solution.py:16
  145.8 7.5 %gather_fusion = bf16[2048,512]{1,0:T(8,128)(2,1)S(1)} fusion(bf16[512,512]{1,0:T(8,128)(2,1)S(1)} %copy-done, s32[2048]{0:T(1024)S(1)} %fusion.2), kind=kCustom, calls=%fused_computation | custom fusion | bytes 4202496 | tf_op jit(solution)/shard_map/jit(_take)/gather | solution.py:68
  153.4 2.4 %copy.14 = bf16[2048,512]{0,1:T(8,128)(2,1)} copy(bf16[2048,512]{1,0:T(8,128)(2,1)S(1)} %gather_fusion) | data formatting | bytes 4194304 | tf_op jit(solution)/shard_map/jit(_take)/gather | solution.py:68
  155.8 0.0 collective-permute-done.5
  155.8 3.2 %collective-permute-start.7 = (bf16[256,512]{1,0:T(8,128)(2,1)S(1)}, bf16[256,512]{1,0:T(8,128)(2,1)S(1)}, u32[]{:S(2)}, u32[]{:S(2)}) collective-permute-start(bf16[256,512]{1,0:T(8,128)(2,1)S(1)} %collective-permute-done.5), channel_id=1, source_target_pairs={{0,28},{4,0},{8,4},{12,8},{16,12},{20,16},{24,20},{28,24},{1,29},{... | collective-permute-start | bytes 786440 | tf_op jit(solution)/shard_map/ppermute | solution.py:21
  158.9 0.1 broadcast_in_dim.26
  159.1 0.0 copy-start.1
  159.1 0.0 collective-permute-done.6
  159.1 0.1 collective-permute-start.8
  159.2 1.1 constant_dynamic-update-slice_fusion.11
  160.3 2.6 %collective-permute-done.7 = bf16[256,512]{1,0:T(8,128)(2,1)S(1)} collective-permute-done((bf16[256,512]{1,0:T(8,128)(2,1)S(1)}, bf16[256,512]{1,0:T(8,128)(2,1)S(1)}, u32[]{:S(2)}, u32[]{:S(2)}) %collective-permute-start.7) | collective-permute-done | bytes 262176 | tf_op jit(solution)/shard_map/ppermute | solution.py:21
  163.0 7.2 %collective-permute-start.9 = (bf16[256,512]{1,0:T(8,128)(2,1)S(1)}, bf16[256,512]{1,0:T(8,128)(2,1)S(1)}, u32[]{:S(2)}, u32[]{:S(2)}) collective-permute-start(bf16[256,512]{1,0:T(8,128)(2,1)S(1)} %collective-permute-done.7), channel_id=1, source_target_pairs={{0,28},{4,0},{8,4},{12,8},{16,12},{20,16},{24,20},{28,24},{1,29},{... | collective-permute-start | bytes 786440 | tf_op jit(solution)/shard_map/ppermute | solution.py:21
  170.2 0.0 collective-permute-done.8
  170.2 0.1 collective-permute-start.10
  170.4 4.4 %collective-permute-done.9 = bf16[256,512]{1,0:T(8,128)(2,1)S(1)} collective-permute-done((bf16[256,512]{1,0:T(8,128)(2,1)S(1)}, bf16[256,512]{1,0:T(8,128)(2,1)S(1)}, u32[]{:S(2)}, u32[]{:S(2)}) %collective-permute-start.9) | collective-permute-done | bytes 262176 | tf_op jit(solution)/shard_map/ppermute | solution.py:21
  174.8 5.0 %collective-permute-done.10 = bf16[256,512]{1,0:T(8,128)(2,1)S(1)} collective-permute-done((bf16[256,512]{1,0:T(8,128)(2,1)S(1)}, bf16[256,512]{1,0:T(8,128)(2,1)S(1)}, u32[]{:S(2)}, u32[]{:S(2)}) %collective-permute-start.10) | collective-permute-done | bytes 262176 | tf_op jit(solution)/shard_map/ppermute | solution.py:16
  179.8 0.0 copy-done.1
  179.8 8.4 %fusion = bf16[2048,512]{0,1:T(8,128)(2,1)S(1)} fusion(bf16[2048,512]{1,0:T(8,128)(2,1)S(1)} %constant_dynamic-update-slice_fusion.5, bf16[2048,2048]{1,0:T(8,128)(2,1)} %param.10, bf16[2048,512]{0,1:T(8,128)(2,1)S(1)} %copy-done.1, pred[2048]{0:T(1024)(128)(4,1)S(1)} %compare_and_fusion), kind=kOutput, calls=%fused_computation.2 | convolution fusion | flops 4299161600 | bytes 14682112 | tf_op jit(solution)/shard_map/dot_general | solution.py:67
  188.2 2.5 %copy.15 = bf16[2048,512]{1,0:T(8,128)(2,1)} copy(bf16[2048,512]{0,1:T(8,128)(2,1)S(1)} %fusion) | data formatting | bytes 4194304 | tf_op jit(solution)/shard_map/convert_element_type | solution.py:69
  (10 shorter events, 0.2 us)
Async XLA Ops:
  0.0 1.0 copy-start
  2.3 30.3 %collective-permute-start = (f32[256,512]{1,0:T(8,128)S(1)}, f32[256,512]{1,0:T(8,128)}, u32[]{:S(2)}, u32[]{:S(2)}) collective-permute-start(f32[256,512]{1,0:T(8,128)S(1)} %fusion.3), channel_id=1, source_target_pairs={} | collective-permute-start | bytes 1572872 | tf_op jit(solution)/shard_map/ppermute | solution.py:31
  3.8 29.9 %collective-permute-start.1 = (f32[256,512]{1,0:T(8,128)S(1)}, f32[256,512]{1,0:T(8,128)}, u32[]{:S(2)}, u32[]{:S(2)}) collective-permute-start(f32[256,512]{1,0:T(8,128)S(1)} %fusion.3), channel_id=1, source_target_pairs={{0,3},{4,7},{8,11},{12,15},{16,19},{20,23},{24,27},{28,31}} | collective-permute-start | bytes 1572872 | tf_op jit(solution)/shard_map/ppermute | solution.py:31
  8.9 25.9 %collective-permute-start.2 = (f32[256,512]{1,0:T(8,128)S(1)}, f32[256,512]{1,0:T(8,128)}, u32[]{:S(2)}, u32[]{:S(2)}) collective-permute-start(f32[256,512]{1,0:T(8,128)S(1)} %fusion.3), channel_id=1, source_target_pairs={{0,2},{1,3},{4,6},{5,7},{8,10},{9,11},{12,14},{13,15},{16,18},{17,... | collective-permute-start | bytes 1572872 | tf_op jit(solution)/shard_map/ppermute | solution.py:31
  11.0 24.8 %collective-permute-start.3 = (f32[256,512]{1,0:T(8,128)S(1)}, f32[256,512]{1,0:T(8,128)}, u32[]{:S(2)}, u32[]{:S(2)}) collective-permute-start(f32[256,512]{1,0:T(8,128)S(1)} %fusion.3), channel_id=1, source_target_pairs={{0,1},{1,2},{2,3},{4,5},{5,6},{6,7},{8,9},{9,10},{10,11},{12,13},{... | collective-permute-start | bytes 1572872 | tf_op jit(solution)/shard_map/ppermute | solution.py:31
  41.7 94.2 %copy-start.2 = (s32[2048]{0:T(1024)S(1)}, s32[2048]{0:T(1024)}, u32[]{:S(2)}) copy-start(s32[2048]{0:T(1024)} %param.11) | copy-start | bytes 24580
  131.2 12.1 %collective-permute-start.4 = (bf16[256,512]{1,0:T(8,128)(2,1)S(1)}, bf16[256,512]{1,0:T(8,128)(2,1)}, u32[]{:S(2)}, u32[]{:S(2)}) collective-permute-start(bf16[256,512]{1,0:T(8,128)(2,1)S(1)} %bitcast.16), channel_id=1, source_target_pairs={{0,4},{4,8},{8,12},{12,16},{16,20},{20,24},{24,28},{28,0},{1,5},{5... | collective-permute-start | bytes 786440 | tf_op jit(solution)/shard_map/ppermute | solution.py:16
  132.7 23.0 %collective-permute-start.5 = (bf16[256,512]{1,0:T(8,128)(2,1)S(1)}, bf16[256,512]{1,0:T(8,128)(2,1)S(1)}, u32[]{:S(2)}, u32[]{:S(2)}) collective-permute-start(bf16[256,512]{1,0:T(8,128)(2,1)S(1)} %bitcast.17), channel_id=1, source_target_pairs={{0,28},{4,0},{8,4},{12,8},{16,12},{20,16},{24,20},{28,24},{1,29},{... | collective-permute-start | bytes 786440 | tf_op jit(solution)/shard_map/ppermute | solution.py:21
  143.2 15.9 %collective-permute-start.6 = (bf16[256,512]{1,0:T(8,128)(2,1)}, bf16[256,512]{1,0:T(8,128)(2,1)S(1)}, u32[]{:S(2)}, u32[]{:S(2)}) collective-permute-start(bf16[256,512]{1,0:T(8,128)(2,1)} %collective-permute-done.4), channel_id=1, source_target_pairs={{0,4},{4,8},{8,12},{12,16},{16,20},{20,24},{24,28},{28,0},{1,5},{5... | collective-permute-start | bytes 786440 | tf_op jit(solution)/shard_map/ppermute | solution.py:16
  155.8 7.2 %collective-permute-start.7 = (bf16[256,512]{1,0:T(8,128)(2,1)S(1)}, bf16[256,512]{1,0:T(8,128)(2,1)S(1)}, u32[]{:S(2)}, u32[]{:S(2)}) collective-permute-start(bf16[256,512]{1,0:T(8,128)(2,1)S(1)} %collective-permute-done.5), channel_id=1, source_target_pairs={{0,28},{4,0},{8,4},{12,8},{16,12},{20,16},{24,20},{28,24},{1,29},{... | collective-permute-start | bytes 786440 | tf_op jit(solution)/shard_map/ppermute | solution.py:21
  159.1 20.7 %copy-start.1 = (bf16[2048,512]{0,1:T(8,128)(2,1)S(1)}, bf16[2048,512]{0,1:T(8,128)(2,1)}, u32[]{:S(2)}) copy-start(bf16[2048,512]{0,1:T(8,128)(2,1)} %copy.14) | copy-start | bytes 6291460
  159.1 11.1 %collective-permute-start.8 = (bf16[256,512]{1,0:T(8,128)(2,1)S(1)}, bf16[256,512]{1,0:T(8,128)(2,1)S(1)}, u32[]{:S(2)}, u32[]{:S(2)}) collective-permute-start(bf16[256,512]{1,0:T(8,128)(2,1)S(1)} %collective-permute-done.6), channel_id=1, source_target_pairs={{0,4},{4,8},{8,12},{12,16},{16,20},{20,24},{24,28},{28,0},{1,5},{5... | collective-permute-start | bytes 786440 | tf_op jit(solution)/shard_map/ppermute | solution.py:16
  163.0 11.8 %collective-permute-start.9 = (bf16[256,512]{1,0:T(8,128)(2,1)S(1)}, bf16[256,512]{1,0:T(8,128)(2,1)S(1)}, u32[]{:S(2)}, u32[]{:S(2)}) collective-permute-start(bf16[256,512]{1,0:T(8,128)(2,1)S(1)} %collective-permute-done.7), channel_id=1, source_target_pairs={{0,28},{4,0},{8,4},{12,8},{16,12},{20,16},{24,20},{28,24},{1,29},{... | collective-permute-start | bytes 786440 | tf_op jit(solution)/shard_map/ppermute | solution.py:21
  170.2 9.5 %collective-permute-start.10 = (bf16[256,512]{1,0:T(8,128)(2,1)S(1)}, bf16[256,512]{1,0:T(8,128)(2,1)S(1)}, u32[]{:S(2)}, u32[]{:S(2)}) collective-permute-start(bf16[256,512]{1,0:T(8,128)(2,1)S(1)} %collective-permute-done.8), channel_id=1, source_target_pairs={{0,4},{4,8},{8,12},{12,16},{16,20},{20,24},{24,28},{28,0},{1,5},{5... | collective-permute-start | bytes 786440 | tf_op jit(solution)/shard_map/ppermute | solution.py:16
